TPU v7x, 32 devices: a whole 2x2x4 slice. The times are simulated.
32 devices in a mesh: row: 4 (over z), col: 4 (over x, core), tm: 2 (over y).
Axes of the slice: x: 2, y: 2, z: 4, core: 2. Of those that a mesh axis runs over, the one named last changes fastest.
Arguments:
- samples: bfloat16 [1024, 4, 2, 16384], P('row', None, 'tm', 'col'), may hold values from -6 to 6
- whitening: bfloat16 [1024, 1024], replicated, may hold values from -0.1875 to 0.1875
- ridge: float32 [2048], P('col'), may hold values from 2 to 20
- slab_start: int32 [1], replicated, may hold values from 0 to 63
- panels: int32 [4], replicated, may hold values from 0 to 3, as said below
Outputs:
- trailing: float32 [131072, 2048], P(('row', 'tm'), 'col')
- factor: bfloat16 [2, 131072, 512], P(None, ('row', 'tm'))
Inputs may be any that keep to these rules, and one draw needn't show every extreme that they name: `panels`: each panel index once.
All inputs are finite; a program needn't handle non-finite values.
Results may differ from a plain program's by a relative error of at most 0.012.
The roundings to bfloat16 on the way count: a program that leaves them out, or rounds other values in their place, can miss the bound.
Values may be sent and summed in bfloat16 or wider, within the bound.
A program may use at most 256 MiB of HBM per device.

v0:
```python
import jax
import jax.numpy as jnp
from jax import lax
from jax.sharding import PartitionSpec as P

S = 1024
PANEL = 512
PANELS = 2


def broadcast(block, axis, holder):
    block = jnp.where(lax.axis_index(axis) == holder, block, jnp.zeros_like(block))
    return lax.psum(block, axis)


def on_device(samples, whitening, ridge, slab_start, panels):
    moved = lax.all_to_all(samples, "row", split_axis=1, concat_axis=0, tiled=True)
    local_width = moved.shape[3]
    series = moved.reshape(moved.shape[0], local_width)
    whitened = jnp.dot(whitening, series, preferred_element_type=jnp.float32).astype(jnp.bfloat16)
    col_count = lax.axis_size("col")
    tm_count = lax.axis_size("tm")
    rows_here = col_count * local_width
    slab_width = PANEL * col_count
    scale = S ** (-0.5)
    slab_first = slab_start[0] * slab_width
    owner_index = slab_first // rows_here
    slab_offset = slab_first % rows_here
    col_index = lax.axis_index("col")
    self_index = lax.axis_index("row") * tm_count + lax.axis_index("tm")
    row_series = lax.all_gather(whitened, "col", axis=1, tiled=True)
    piece = lax.dynamic_slice_in_dim(row_series, slab_offset + col_index * PANEL, PANEL, 1)
    slab_part = broadcast(piece, ("row", "tm"), owner_index)
    covariance = (
        lax.dot_general(
            row_series, slab_part, (((0,), (0,)), ((), ())), preferred_element_type=jnp.float32
        )
        * scale
    )
    owner_flag = (self_index == owner_index).astype(jnp.float32)
    ridge_rows = slab_offset + col_index * PANEL
    zero_index = jnp.zeros((), jnp.int32)
    diag_block = (
        lax.dynamic_slice(covariance, (ridge_rows, zero_index), (PANEL, PANEL))
        + jnp.diag(ridge) * owner_flag
    )
    covariance = lax.dynamic_update_slice(covariance, diag_block, (ridge_rows, zero_index))
    identity = jnp.eye(PANEL, dtype=jnp.float32)
    factors = []
    finished = col_index < 0
    for section in range(PANELS):
        panel_index = panels[section]
        finished = finished | (col_index == panel_index)
        pivot_local = lax.dynamic_slice_in_dim(
            covariance, slab_offset + panel_index * PANEL, PANEL, 0
        )
        pivot_rows = broadcast(pivot_local, ("row", "tm"), owner_index)
        pivot_safe = jnp.where(col_index == panel_index, pivot_rows, identity)
        lower_factor = jnp.linalg.cholesky(pivot_safe)
        panel_now = jax.scipy.linalg.solve_triangular(lower_factor, covariance.T, lower=True).T
        small_block = lower_factor
        panel_bf = broadcast(panel_now.astype(jnp.bfloat16), "col", panel_index)
        small_block = broadcast(small_block, "col", panel_index)
        coupling = jax.scipy.linalg.solve_triangular(small_block, pivot_rows, lower=True).T
        coupling_bf = coupling.astype(jnp.bfloat16)
        covariance = covariance - lax.dot_general(
            panel_bf, coupling_bf, (((1,), (1,)), ((), ())), preferred_element_type=jnp.float32
        )
        factors.append(panel_bf)
    trailing = jnp.where(finished, jnp.zeros_like(covariance), covariance)
    return (trailing, jnp.stack(factors))


def solution(mesh):
    in_specs = (P("row", None, "tm", "col"), P(), P("col"), P(), P())
    out_specs = (P(("row", "tm"), "col"), P(None, ("row", "tm"), None))
    return jax.shard_map(
        on_device, mesh=mesh, in_specs=in_specs, out_specs=out_specs, check_vma=False
    )
```

profile of v0, /device:TPU:0, one launch (start us, length us, event | category | flops | bytes accessed | tf_op | source)
XLA Modules:
  0.0 1940.7 jit_solution(8248852513893661534)
XLA Ops:
  18.7 189.4 %all_to_all.15 = bf16[256,4,1,4096]{3,0,2,1:T(8,128)(2,1)S(1)} all-to-all(bf16[256,4,1,4096]{3,0,2,1:T(8,128)(2,1)} %copy.58), channel_id=1, replica_groups=mesh['row'=4,'col'=4,'tm'=2] {'row'}, dimensions={1} | all-to-all | bytes 16777216 | tf_op jit(solution)/shard_map/all_to_all | solution.py:17
  219.7 200.6 %all-gather.2.cloned.1.call-done = bf16[1024,16384]{1,0:T(8,128)(2,1)} async-done(((bf16[1024,4096]{1,0:T(8,128)(2,1)}), bf16[1024,16384]{1,0:T(8,128)(2,1)}) %all-gather.2.cloned.1.call-update) | async-done | bytes 33554448 | tf_op jit(solution)/shard_map/all_gather | solution.py:31
  424.9 77.7 %all-reduce.9.cloned.1.call-done = bf16[1024,512]{1,0:T(8,128)(2,1)} async-done(((bf16[1024,512]{1,0:T(8,128)(2,1)}), bf16[1024,512]{1,0:T(8,128)(2,1)}) %all-reduce.9.cloned.1.call-update) | async-done | bytes 1048592 | tf_op jit(solution)/shard_map/psum | solution.py:13
  502.6 31.8 %convolution_multiply_fusion = f32[16384,512]{0,1:T(8,128)} fusion(bf16[1024,16384]{1,0:T(8,128)(2,1)} %all-gather.2.cloned.1.call-done, bf16[1024,512]{1,0:T(8,128)(2,1)} %all-reduce.9.cloned.1.call-done), kind=kOutput, calls=%fused_computation.12 | convolution fusion | flops 17188257792 | bytes 68157440 | tf_op jit(solution)/shard_map/dot_general | solution.py:35
  545.3 77.2 %all-reduce.11.cloned.1.call-done = f32[512,512]{0,1:T(8,128)} async-done(((f32[512,512]{0,1:T(8,128)}), f32[512,512]{0,1:T(8,128)}) %all-reduce.11.cloned.1.call-update) | async-done | bytes 1048592 | tf_op jit(solution)/shard_map/psum | solution.py:13
  717.9 39.3 %custom-call.34 = f32[4,128,128]{1,2,0:T(8,128)S(1)} custom-call(f32[4,128,128]{2,1,0:T(8,128)S(1)} %get-tuple-element.33), custom_call_target="InvertDiagBlocksLowerTriangular" | custom-call | tf_op jit(solution)/shard_map/jit(_solve_triangular)/triangular_solve | solution.py:60
  789.4 16.6 convolution_subtract_fusion.3
  817.7 22.9 %fusion.15 = f32[128,16384]{1,0:T(8,128)} fusion(f32[128,16384]{1,0:T(8,128)} %fusion.96, f32[128,16384]{1,0:T(8,128)} %fusion.98, f32[128,16384]{1,0:T(8,128)} %copy-done.2, f32[512,16384]{1,0:T(8,128)} %bitcast.173, f32[512,512]{0,1:T(8,128)S(1)} %get-tuple-element.357), kind=kOutput, calls=%fused_computation.31 | convolution fusion | flops 9678356480 | bytes 42139648 | tf_op jit(solution)/shard_map/jit(_solve_triangular)/triangular_solve | solution.py:60
  851.8 17.2 fusion.21
  879.7 39.3 %custom-call.35 = f32[4,128,128]{1,2,0:T(8,128)S(1)} custom-call(f32[4,128,128]{2,1,0:T(8,128)S(1)} %get-tuple-element.34), custom_call_target="InvertDiagBlocksLowerTriangular" | custom-call | tf_op jit(solution)/shard_map/jit(_solve_triangular)/triangular_solve | solution.py:64
  923.8 233.6 %all-reduce.13.cloned.1.call-done = bf16[16384,512]{0,1:T(8,128)(2,1)} async-done(((bf16[16384,512]{0,1:T(8,128)(2,1)}), bf16[16384,512]{0,1:T(8,128)(2,1)}) %all-reduce.13.cloned.1.call-update) | async-done | bytes 16777232 | tf_op jit(solution)/shard_map/psum | solution.py:13
  1157.4 28.8 %convolution_subtract_fusion = f32[16384,512]{0,1:T(8,128)} fusion(f32[16384,512]{0,1:T(8,128)} %dynamic_update_slice.3, bf16[16384,512]{0,1:T(8,128)(2,1)} %all-reduce.13.cloned.1.call-done, bf16[128,512]{1,0:T(8,128)(2,1)S(1)} %fusion.91, f32[128,512]{1,0:T(8,128)S(1)} %fusion.92, f32[128,512]{1,0:T(8,128)S(1)} %fusion.94, f32[128,512]{1,0:T(8,128)S(1)} %fusion.60), kind=kOutput, calls=%fused_computation.25 | convolution fusion | flops 8600420352 | bytes 84803584 | tf_op jit(solution)/shard_map/dot_general | solution.py:66
  1189.7 77.6 %all-reduce.17.cloned.1.call-done = f32[512,512]{0,1:T(8,128)} async-done(((f32[512,512]{0,1:T(8,128)}), f32[512,512]{0,1:T(8,128)}) %all-reduce.17.cloned.1.call-update) | async-done | bytes 1048592 | tf_op jit(solution)/shard_map/psum | solution.py:13
  1363.2 39.3 %custom-call.39 = f32[4,128,128]{1,2,0:T(8,128)S(1)} custom-call(f32[4,128,128]{2,1,0:T(8,128)S(1)} %get-tuple-element.35), custom_call_target="InvertDiagBlocksLowerTriangular" | custom-call | tf_op jit(solution)/shard_map/jit(_solve_triangular)/triangular_solve | solution.py:60
  1412.3 12.8 convolution_subtract_fusion.2
  1434.7 16.7 convolution_subtract_fusion.1
  1463.0 22.9 %fusion.12 = f32[128,16384]{1,0:T(8,128)} fusion(f32[128,16384]{1,0:T(8,128)} %fusion.86, f32[128,16384]{1,0:T(8,128)} %fusion.88, f32[128,16384]{1,0:T(8,128)} %copy-done.3, f32[512,16384]{1,0:T(8,128)} %bitcast.169, f32[512,512]{0,1:T(8,128)S(1)} %get-tuple-element.358), kind=kOutput, calls=%fused_computation.30 | convolution fusion | flops 9678356480 | bytes 42139648 | tf_op jit(solution)/shard_map/jit(_solve_triangular)/triangular_solve | solution.py:60
  1497.1 17.2 fusion.19
  1524.0 39.5 %custom-call.40 = f32[4,128,128]{1,2,0:T(8,128)S(1)} custom-call(f32[4,128,128]{2,1,0:T(8,128)S(1)} %get-tuple-element.36), custom_call_target="InvertDiagBlocksLowerTriangular" | custom-call | tf_op jit(solution)/shard_map/jit(_solve_triangular)/triangular_solve | solution.py:64
  1568.3 235.2 %all-reduce.19.cloned.1.call-done = bf16[16384,512]{0,1:T(8,128)(2,1)} async-done(((bf16[16384,512]{0,1:T(8,128)(2,1)}), bf16[16384,512]{0,1:T(8,128)(2,1)}) %all-reduce.19.cloned.1.call-update) | async-done | bytes 16777232 | tf_op jit(solution)/shard_map/psum | solution.py:13
  1803.5 29.5 %subtract_select_fusion = f32[16384,512]{0,1:T(8,128)} fusion(f32[16384,512]{0,1:T(8,128)} %convolution_subtract_fusion, bf16[16384,512]{0,1:T(8,128)(2,1)} %all-reduce.19.cloned.1.call-done, pred[]{:T(512)S(6)} %or.26, bf16[128,512]{1,0:T(8,128)(2,1)S(1)} %fusion.81, f32[128,512]{1,0:T(8,128)S(1)} %fusion.82, f32[128,512]{1,0:T(8,128)S(1)} %fusion.84, ...), kind=kOutput, calls=%fused_computation.11 | convolution fusion | flops 8608808960 | bytes 84803584 | tf_op jit(solution)/shard_map/dot_general | solution.py:66
  1833.1 33.4 %copy.88 = f32[16384,512]{1,0:T(8,128)} copy(f32[16384,512]{0,1:T(8,128)} %subtract_select_fusion) | data formatting | bytes 67108864
  1866.5 23.0 %pad_maximum_fusion = bf16[2,16384,512]{1,2,0:T(8,128)(2,1)} fusion(bf16[1,16384,512]{1,2,0:T(8,128)(2,1)} %bitcast.175, bf16[1,16384,512]{1,2,0:T(8,128)(2,1)} %bitcast.174), kind=kLoop, calls=%fused_computation.10 | loop fusion | flops 16777216 | bytes 67108864 | tf_op jit(solution)/shard_map/stack | solution.py:71
  1889.5 44.1 %copy.89 = bf16[2,16384,512]{2,1,0:T(8,128)(2,1)} copy(bf16[2,16384,512]{1,2,0:T(8,128)(2,1)} %pad_maximum_fusion) | data formatting | bytes 67108864
  (232 shorter events, 385.1 us)
Async XLA Ops:
  7.2 200.9 %copy-start = (bf16[1024,1024]{1,0:T(8,128)(2,1)S(1)}, bf16[1024,1024]{1,0:T(8,128)(2,1)}, u32[]{:S(2)}) copy-start(bf16[1024,1024]{1,0:T(8,128)(2,1)} %param.11) | copy-start | bytes 6291460
  7.2 413.1 %all-gather.2.cloned.1.call-start = ((), (), s32[]{:S(2)}) async-start(), calls=%async_computation.1 | async-start | bytes 41943040 | tf_op jit(solution)/shard_map/all_gather | solution.py:31
  218.9 204.7 %copy-start.7 = (s32[4]{0:T(128)S(1)}, s32[4]{0:T(128)}, u32[]{:S(2)}) copy-start(s32[4]{0:T(128)} %param.14) | copy-start | bytes 52
  218.9 283.7 %all-reduce.9.cloned.1.call-start = ((), (), s32[]{:S(2)}) async-start(), calls=%async_computation.2 | async-start | bytes 2097152 | tf_op jit(solution)/shard_map/psum | solution.py:13
  423.1 199.4 %all-reduce.11.cloned.1.call-start = ((), (), s32[]{:S(2)}) async-start(), calls=%async_computation.3 | async-start | bytes 2097152 | tf_op jit(solution)/shard_map/psum | solution.py:13
  424.9 109.4 %copy-start.6 = (f32[512]{0:T(512)S(1)}, f32[512]{0:T(512)}, u32[]{:S(2)}) copy-start(f32[512]{0:T(512)} %param.12) | copy-start | bytes 6148
  544.5 325.3 %all-reduce.15.cloned.1.call-start = ((), (), s32[]{:S(2)}) async-start(), calls=%async_computation.5 | async-start | bytes 2097152 | tf_op jit(solution)/shard_map/psum | solution.py:13
  757.2 400.2 %all-reduce.13.cloned.1.call-start = ((), (), s32[]{:S(2)}) async-start(), calls=%async_computation.4 | async-start | bytes 33554432 | tf_op jit(solution)/shard_map/psum | solution.py:13
  767.0 12.8 copy-start.2
  868.9 50.0 %copy-start.4 = (f32[512,512]{0,1:T(8,128)S(1)}, f32[512,512]{0,1:T(8,128)}, u32[]{:S(2)}) copy-start(f32[512,512]{0,1:T(8,128)} %all-reduce.11.cloned.1.call-done) | copy-start | bytes 3145732
  869.0 398.3 %all-reduce.17.cloned.1.call-start = ((), (), s32[]{:S(2)}) async-start(), calls=%async_computation.6 | async-start | bytes 2097152 | tf_op jit(solution)/shard_map/psum | solution.py:13
  1188.8 325.5 %all-reduce.21.cloned.1.call-start = ((), (), s32[]{:S(2)}) async-start(), calls=%async_computation.8 | async-start | bytes 2097152 | tf_op jit(solution)/shard_map/psum | solution.py:13
  1402.5 401.0 %all-reduce.19.cloned.1.call-start = ((), (), s32[]{:S(2)}) async-start(), calls=%async_computation.7 | async-start | bytes 33554432 | tf_op jit(solution)/shard_map/psum | solution.py:13
  1412.3 12.8 copy-start.3
  1514.3 49.2 %copy-start.5 = (f32[512,512]{0,1:T(8,128)S(1)}, f32[512,512]{0,1:T(8,128)}, u32[]{:S(2)}) copy-start(f32[512,512]{0,1:T(8,128)} %all-reduce.17.cloned.1.call-done) | copy-start | bytes 3145732
  1889.5 44.1 %copy-start.1 = (bf16[1024,1024]{1,0:T(8,128)(2,1)S(1)}, bf16[1024,1024]{1,0:T(8,128)(2,1)}, u32[]{:S(2)}) copy-start(bf16[1024,1024]{1,0:T(8,128)(2,1)} %param.11) | copy-start | bytes 6291460
Sparse Core Ops, SparseCore 0:
  219.1 201.1 all-gather.1
  424.3 78.2 all-reduce.8
  544.6 77.8 all-reduce.10
  757.3 36.2 all-reduce.14
  869.1 288.2 all-reduce.12
  1189.0 78.2 all-reduce.16
  1402.6 37.1 all-reduce.20
  1514.4 289.0 all-reduce.18
where the time goes:
time: 1950 us; the launch traced here: 1940 us
  waiting for transfers between devices  902 us (46%)
  other arithmetic  389 us (20%)
  matrix products  304 us (16%)
  blocking collectives  189 us (10%)
  local copies, waits for them, and re-layouts  131 us (7%)
  between operations  23.4 us (1%)
    psum x7, waiting for transfers between devices, broadcast(): return lax.psum(block, axis)  701 us
    all_gather x1, waiting for transfers between devices, on_device(): row_series = lax.all_gather(whitened, 'col', axis=1, tiled=True)  201 us
    all_to_all x1, blocking collectives, on_device(): lax.all_to_all(samples, 'row', split_axis=1, concat_axis=0, tiled=True)  189 us
    another operation x14, matrix products, on_device(): jax.scipy.linalg.solve_triangular(lower_factor, covariance.T, lower=True)  189 us
    another operation x29, other arithmetic, on_device(): lower_factor = jnp.linalg.cholesky(pivot_safe)  159 us
    unnamed x19, local copies, waits for them, and re-layouts  89.1 us
    another operation x4, other arithmetic, on_device(): jax.scipy.linalg.solve_triangular(small_block, pivot_rows, lower=True)  81.5 us
    another operation x3, other arithmetic, on_device(): jax.scipy.linalg.solve_triangular(lower_factor, covariance.T, lower=True)  78.6 us
  transfers between devices with their start and end apart: 8, of which 6 were waited for; matrix products, arithmetic and copies ran while one was open for 17% of the time, Pallas kernels for 0%

commit v1 on v0

v1 whole, which is shorter than its diff:
```python
import functools
import math
import jax
import jax.numpy as jnp
from jax import lax
from jax.experimental import pallas as pl
from jax.experimental.pallas import tpu as pltpu
from jax.sharding import PartitionSpec as P

NB = 128
SUB = 8
HIGH = lax.Precision.HIGHEST


def block_inverse(a):
    n = NB // SUB
    rows = [a[s * SUB:(s + 1) * SUB, :] for s in range(n)]
    lane = lax.broadcasted_iota(jnp.int32, (SUB, NB), 1)
    sub = lax.broadcasted_iota(jnp.int32, (SUB, NB), 0)
    inv = [jnp.where(lane == sub + s * SUB, 1.0, 0.0).astype(jnp.float32) for s in range(n)]
    for k in range(NB):
        s0, r = divmod(k, SUB)
        row_a = rows[s0][r:r + 1, :]
        row_v = inv[s0][r:r + 1, :]
        scale = 1.0 / row_a[:, k:k + 1]
        row_a_s = row_a * scale
        row_v_s = row_v * scale
        for s in range(s0, n):
            column = jnp.broadcast_to(rows[s][:, k:k + 1], (SUB, NB))
            if s == s0:
                if r == SUB - 1:
                    continue
                column = jnp.where(sub > r, column, 0.0)
            rows[s] = rows[s] - column * row_a_s
            inv[s] = inv[s] - column * row_v_s
    out = []
    for s in range(n):
        d = jnp.sum(jnp.where(lane == sub + s * SUB, rows[s], 0.0), axis=1, keepdims=True)
        out.append(inv[s] / jnp.sqrt(d))
    return jnp.concatenate(out, axis=0)


def inverse_kernel(a_ref, o_ref, work):
    size = a_ref.shape[0]
    work[:, :size] = a_ref[...]
    ri = lax.broadcasted_iota(jnp.int32, (size, size), 0)
    ci = lax.broadcasted_iota(jnp.int32, (size, size), 1)
    work[:, size:] = jnp.where(ri == ci, 1.0, 0.0).astype(jnp.float32)
    row_id = lax.broadcasted_iota(jnp.int32, (size, 1), 0)

    def step(b, carry):
        at = pl.multiple_of(b * NB, NB)
        small = block_inverse(work[pl.ds(at, NB), pl.ds(at, NB)])
        top = jnp.dot(small, work[pl.ds(at, NB), :], preferred_element_type=jnp.float32, precision=HIGH)
        left = jnp.where(row_id >= at + NB, top[:, :size].T, 0.0)
        update = jnp.dot(left, top, preferred_element_type=jnp.float32, precision=HIGH)
        work[...] = work[...] - update
        work[pl.ds(at, NB), :] = top
        return carry

    lax.fori_loop(0, size // NB, step, 0)
    o_ref[...] = work[:, size:]


def lower_inverse(a):
    size = a.shape[0]
    return pl.pallas_call(
        inverse_kernel,
        out_shape=jax.ShapeDtypeStruct((size, size), jnp.float32),
        in_specs=[pl.BlockSpec(memory_space=pltpu.VMEM)],
        out_specs=pl.BlockSpec(memory_space=pltpu.VMEM),
        scratch_shapes=[pltpu.VMEM((size, 2 * size), jnp.float32)],
        compiler_params=pltpu.CompilerParams(vmem_limit_bytes=40 * 2**20),
        name="lower_inverse",
    )(a)


def final_kernel(bm, chunk_base, info, x_ref, m_ref, d0_ref, d1_ref, dn_ref, *rest):
    t_ref, f_ref = rest[-2:]
    width = t_ref.shape[1]
    acc = jnp.dot(x_ref[...], m_ref[...], preferred_element_type=jnp.float32)
    block = chunk_base(pl.program_id(0), pl.program_id(1))
    inside = (block >= info[0]) & (block < info[1])

    @pl.when(inside)
    def _():
        f_ref[0] = (acc[:, :width] + d0_ref[...]).astype(f_ref.dtype)
        f_ref[1] = (acc[:, width:2 * width] + d1_ref[...]).astype(f_ref.dtype)
        t_ref[...] = acc[:, 2 * width:] + dn_ref[...]

    @pl.when(jnp.logical_not(inside))
    def _():
        f_ref[0] = acc[:, :width].astype(f_ref.dtype)
        f_ref[1] = acc[:, width:2 * width].astype(f_ref.dtype)
        t_ref[...] = acc[:, 2 * width:]


def final_chunk(info, x, weights, d0, d1, dn, prior, chunk, chunks, cols, local, width, bm):
    w = local // chunks
    per = w // bm
    rows = cols * local
    depth = x.shape[1]

    def base(c, i):
        return c * (local // bm) + chunk * per + i

    def d_map(c, i, info):
        block = base(c, i)
        inside = (block >= info[0]) & (block < info[1])
        return (jnp.where(inside, block - info[0], 0), 0)

    in_specs = [
        pl.BlockSpec((bm, depth), lambda c, i, info: (c * per + i, 0)),
        pl.BlockSpec((depth, 3 * width), lambda c, i, info: (0, 0)),
        pl.BlockSpec((bm, width), d_map),
        pl.BlockSpec((bm, width), d_map),
        pl.BlockSpec((bm, width), d_map),
    ]
    operands = [info, x, weights, d0, d1, dn]
    aliases = {}
    if prior is not None:
        in_specs += [pl.BlockSpec(memory_space=pl.ANY)] * 2
        operands += list(prior)
        aliases = {6: 0, 7: 1}
    return pl.pallas_call(
        functools.partial(final_kernel, bm, base),
        grid_spec=pltpu.PrefetchScalarGridSpec(
            num_scalar_prefetch=1,
            grid=(cols, per),
            in_specs=in_specs,
            out_specs=[
                pl.BlockSpec((bm, width), lambda c, i, info: (base(c, i), 0)),
                pl.BlockSpec((2, bm, width), lambda c, i, info: (0, base(c, i), 0)),
            ],
        ),
        out_shape=[
            jax.ShapeDtypeStruct((rows, width), jnp.float32),
            jax.ShapeDtypeStruct((2, rows, width), jnp.bfloat16),
        ],
        input_output_aliases=aliases,
        compiler_params=pltpu.CompilerParams(
            vmem_limit_bytes=48 * 2**20, dimension_semantics=("arbitrary", "arbitrary")
        ),
        name="final",
    )(*operands)


def high(a, b, dims):
    return lax.dot_general(a, b, ((dims[:1], dims[1:]), ((), ())), preferred_element_type=jnp.float32, precision=HIGH)


def on_device(samples, whitening, ridge, slab_start, panels):
    times, groups, _, local = samples.shape
    cols = lax.axis_size("col")
    tms = lax.axis_size("tm")
    width = ridge.shape[0]
    slab = width * cols
    kd = local * cols
    depth = whitening.shape[0]
    scale = 1.0 / math.sqrt(depth)
    me_col = lax.axis_index("col")
    me_tm = lax.axis_index("tm")
    me_row = lax.axis_index("row")

    first = slab_start[0] * slab
    group = first // (tms * kd)
    tm_owner = (first % (tms * kd)) // kd
    offset = first % kd

    mine = lax.dynamic_index_in_dim(samples[:, :, 0], group, 1, keepdims=False)
    pieces = []
    for p in range(cols):
        at = offset + p * width
        have = (me_tm == tm_owner) & (me_col == at // local)
        part = lax.dynamic_slice_in_dim(mine, at % local, width, 1)
        pieces.append(jnp.where(have, part, jnp.zeros_like(part)))
    raw = lax.psum(jnp.concatenate(pieces, axis=1), ("tm", "col"))
    raw = lax.all_gather(raw, "row", axis=0, tiled=True)
    ridge_all = lax.all_gather(ridge, "col", axis=0, tiled=True)

    chunks = 4 if local >= 4096 else 2
    w = local // chunks
    gathered = []
    for c in range(chunks):
        moved = lax.all_to_all(samples[:, :, :, c * w:(c + 1) * w], "row", split_axis=1, concat_axis=0, tiled=True)
        moved = moved.reshape(depth, w)
        series = lax.dot_general(
            moved, whitening, (((0,), (1,)), ((), ())), preferred_element_type=jnp.float32
        ).astype(jnp.bfloat16)
        gathered.append(lax.all_gather(series, "col", axis=0, tiled=True))

    sw = jnp.dot(whitening, raw, preferred_element_type=jnp.float32).astype(jnp.bfloat16)
    cut = lambda q: lax.dynamic_slice_in_dim(sw, q * width, width, 1)
    q0, q1 = panels[0], panels[1]
    s0, s1, sj = cut(q0), cut(q1), cut(me_col)
    r0 = lax.dynamic_slice_in_dim(ridge_all, q0 * width, width, 0)
    r1 = lax.dynamic_slice_in_dim(ridge_all, q1 * width, width, 0)
    both = jnp.concatenate([s0, s1], axis=1)
    gram = lax.dot_general(
        both, jnp.concatenate([both, sj], axis=1), (((0,), (0,)), ((), ())), preferred_element_type=jnp.float32
    ) * scale
    own0 = (q0 == me_col).astype(jnp.float32)
    own1 = (q1 == me_col).astype(jnp.float32)
    a00 = gram[:width, :width] + jnp.diag(r0)
    a01 = gram[:width, width:2 * width]
    a0j = gram[:width, 2 * width:] + jnp.diag(r0) * own0
    a11 = gram[width:, width:2 * width] + jnp.diag(r1)
    a1j = gram[width:, 2 * width:] + jnp.diag(r1) * own1
    i0 = lower_inverse(a00)
    c0 = high(i0, jnp.concatenate([a01, a0j], axis=1), (1, 0)).astype(jnp.bfloat16)
    c01, c0j = c0[:, :width], c0[:, width:]
    fix = lax.dot_general(c01, c0, (((0,), (0,)), ((), ())), preferred_element_type=jnp.float32)
    i1 = lower_inverse(a11 - fix[:, :width])
    c1j = high(i1, a1j - fix[:, width:], (1, 0)).astype(jnp.bfloat16)

    zero = jnp.zeros((width, width), jnp.float32)
    e0 = jnp.diag(r0)
    e1 = jnp.diag(r1)
    m0 = high(jnp.concatenate([s0.astype(jnp.float32) * scale, e0], axis=0), i0, (1, 1))
    m0z = jnp.concatenate([m0, zero], axis=0)
    t1 = jnp.concatenate([s1.astype(jnp.float32) * scale, zero, e1], axis=0) - high(
        m0z, c01.astype(jnp.float32), (1, 0))
    m1 = high(t1, i1, (1, 1))
    base = jnp.concatenate([sj.astype(jnp.float32) * scale, zero, zero], axis=0)
    n = base - high(m0z, c0j.astype(jnp.float32), (1, 0)) - high(m1, c1j.astype(jnp.float32), (1, 0))
    finished = (me_col == q0) | (me_col == q1)
    n = jnp.where(finished, 0.0, n)
    weights = jnp.concatenate([m0[:depth], m1[:depth], n[:depth]], axis=1).astype(jnp.bfloat16)

    def spread(rows):
        out = jnp.zeros((slab, width), jnp.float32)
        out = lax.dynamic_update_slice(out, rows[:width], (q0 * width, jnp.zeros((), jnp.int32)))
        return lax.dynamic_update_slice(out, rows[width:], (q1 * width, jnp.zeros((), jnp.int32)))

    d0 = spread(m0z[depth:])
    d1 = spread(m1[depth:])
    own_ridge = jnp.where(finished, 0.0, jnp.diag(ridge))
    dn = spread(n[depth:])
    zi = jnp.zeros((), jnp.int32)
    at = (me_col * width, zi)
    dn = lax.dynamic_update_slice(dn, lax.dynamic_slice(dn, at, (width, width)) + own_ridge, at)

    bm = min(512, w)
    owner = (me_row == group) & (me_tm == tm_owner)
    low_block = offset // bm
    info = jnp.stack([
        jnp.where(owner, low_block, 0),
        jnp.where(owner, low_block + slab // bm, 0),
    ]).astype(jnp.int32)
    prior = None
    for c in range(chunks):
        prior = final_chunk(info, gathered[c], weights, d0, d1, dn, prior, c, chunks, cols, local, width, bm)
    return tuple(prior)


def solution(mesh):
    in_specs = (P("row", None, "tm", "col"), P(), P("col"), P(), P())
    out_specs = (P(("row", "tm"), "col"), P(None, ("row", "tm"), None))
    return jax.shard_map(
        on_device, mesh=mesh, in_specs=in_specs, out_specs=out_specs, check_vma=False
    )
```

time: 1950 us -> 655 us (0.34)
  waiting for transfers between devices: 902 us -> 59.6 us
  other arithmetic: 389 us -> 7.53 us
  matrix products: 304 us -> 58.1 us
  Pallas kernels: 0 us -> 187 us
  local copies, waits for them, and re-layouts: 131 us -> 49.1 us
  blocking collectives: 189 us -> 265 us
    psum x7 -> x1, waiting for transfers between devices: 701 us -> 59.5 us  [on_device(): raw = lax.psum(jnp.concatenate(pieces, axis=1), ('tm', 'col'))]
    another operation x37 -> x1, other arithmetic: 342 us -> 0.07 us  [on_device(): jnp.stack([jnp.where(owner, low_block, 0), jnp.where(owner, low_block + s...]
    another operation x40 -> x0, matrix products: 203 us -> none  [the longest x14 189 us: on_device(): jax.scipy.linalg.solve_triangular(lower_factor, covariance.T, lower=True)]
    all_gather x1 -> x5, waiting for transfers between devices: 201 us -> 0.03 us  [the longest x4 0.03 us: on_device(): gathered.append(lax.all_gather(series, 'col', axis=0, tiled=True))]
    pallas_call x0 -> x6, Pallas kernels: none -> 187 us  [the longest x2 105 us: lower_inverse(): pl.pallas_call(inverse_kernel, out_shape=jax.ShapeDtypeStruct((size, size...]
    all_to_all x1 -> x4, blocking collectives: 189 us -> 260 us  [on_device(): lax.all_to_all(samples[:, :, :, c * w:(c + 1) * w], 'row', split_axis=1,...]
    unnamed x19 -> x57, local copies, waits for them, and re-layouts: 89.1 us -> 24.3 us
    select_n x9 -> x5, other arithmetic: 45.1 us -> 0.51 us  [the longest x1 0.34 us: on_device(): e1 = jnp.diag(r1)]
  transfers between devices with their start and end apart: 8 -> 6, of which waited for: 6 -> 1; matrix products, arithmetic and copies ran while one was open for 17% -> 15% of each run, Pallas kernels for 0% -> 26%
where the time goes in v1:
time: 655 us; the launch traced here: 647 us
  blocking collectives  265 us (40%)
  Pallas kernels  187 us (29%)
  waiting for transfers between devices  59.6 us (9%)
  matrix products  58.1 us (9%)
  local copies, waits for them, and re-layouts  49.1 us (7%)
  between operations  20 us (3%)
  other arithmetic  7.53 us (1%)
    all_to_all x4, blocking collectives, on_device(): lax.all_to_all(samples[:, :, :, c * w:(c + 1) * w], 'row', split_axis=1,...  260 us
    pallas_call x2, Pallas kernels, lower_inverse(): pl.pallas_call(inverse_kernel, out_shape=jax.ShapeDtypeStruct((size, size...  105 us
    pallas_call x4, Pallas kernels, final_chunk(): pl.pallas_call(functools.partial(final_kernel, bm, base), grid_spec=pltpu...  82.3 us
    psum x1, waiting for transfers between devices, on_device(): raw = lax.psum(jnp.concatenate(pieces, axis=1), ('tm', 'col'))  59.5 us
    dot_general x7, matrix products, high(): lax.dot_general(a, b, ((dims[:1], dims[1:]), ((), ())), preferred_element...  32.2 us
    unnamed x57, local copies, waits for them, and re-layouts  24.3 us
    dot_general x4, matrix products, on_device(): lax.dot_general(moved, whitening, (((0,), (1,)), ((), ())), preferred_ele...  14.8 us
  transfers between devices with their start and end apart: 6, of which 1 were waited for; matrix products, arithmetic and copies ran while one was open for 15% of the time, Pallas kernels for 26%

profile of v1, /device:TPU:0, one launch (start us, length us, event | category | flops | bytes accessed | tf_op | source)
XLA Modules:
  0.0 647.1 jit_solution(1583891098985764200)
XLA Ops:
  8.3 6.4 constant_dynamic-slice_fusion.3
  16.0 59.5 %all-reduce.4.cloned.1.call-done = bf16[256,2048]{1,0:T(8,128)(2,1)} async-done(((bf16[256,2048]{1,0:T(8,128)(2,1)}), bf16[256,2048]{1,0:T(8,128)(2,1)}) %all-reduce.4.cloned.1.call-update) | async-done | bytes 1048592 | tf_op jit(solution)/shard_map/psum | solution.py:177
  75.6 6.4 fusion.52
  82.7 107.7 %all_to_all.60 = bf16[256,4,1,1024]{3,0,2,1:T(8,128)(2,1)S(1)} all-to-all(bf16[256,4,1,1024]{3,0,2,1:T(8,128)(2,1)S(1)} %copy.67), channel_id=1, replica_groups=mesh['row'=4,'col'=4,'tm'=2] {'row'}, dimensions={1} | all-to-all | bytes 4194304 | tf_op jit(solution)/shard_map/all_to_all | solution.py:185
  190.4 3.7 convolution_convert_fusion.1
  196.4 51.4 %all_to_all.61 = bf16[256,4,1,1024]{3,0,2,1:T(8,128)(2,1)S(1)} all-to-all(bf16[256,4,1,1024]{3,0,2,1:T(8,128)(2,1)S(1)} %copy.66), channel_id=1, replica_groups=mesh['row'=4,'col'=4,'tm'=2] {'row'}, dimensions={1} | all-to-all | bytes 4194304 | tf_op jit(solution)/shard_map/all_to_all | solution.py:185
  247.8 3.7 convolution_convert_fusion.2
  253.9 50.4 %all_to_all.62 = bf16[256,4,1,1024]{3,0,2,1:T(8,128)(2,1)S(1)} all-to-all(bf16[256,4,1,1024]{3,0,2,1:T(8,128)(2,1)S(1)} %copy.65), channel_id=1, replica_groups=mesh['row'=4,'col'=4,'tm'=2] {'row'}, dimensions={1} | all-to-all | bytes 4194304 | tf_op jit(solution)/shard_map/all_to_all | solution.py:185
  304.3 3.7 convolution_convert_fusion.3
  310.3 50.3 %all_to_all.63 = bf16[256,4,1,1024]{3,0,2,1:T(8,128)(2,1)S(1)} all-to-all(bf16[256,4,1,1024]{3,0,2,1:T(8,128)(2,1)S(1)} %copy.60), channel_id=1, replica_groups=mesh['row'=4,'col'=4,'tm'=2] {'row'}, dimensions={1} | all-to-all | bytes 4194304 | tf_op jit(solution)/shard_map/all_to_all | solution.py:185
  360.5 3.7 convolution_convert_fusion.4
  368.8 5.6 all-gather
  374.5 6.9 %convolution_convert_fusion = bf16[2048,1024]{0,1:T(8,128)(2,1)S(1)} fusion(bf16[1024,1024]{1,0:T(8,128)(2,1)S(1)} %copy-done, bf16[1024,2048]{1,0:T(8,128)(2,1)} %all-gather.9.cloned.1.call-done), kind=kOutput, calls=%fused_computation.12 | convolution fusion | flops 4297064448 | bytes 10485760 | tf_op jit(solution)/shard_map/dot_general | solution.py:192
  387.8 52.6 %lower_inverse.2 = f32[512,512]{1,0:T(8,128)S(1)} custom-call(f32[512,512]{1,0:T(8,128)S(1)} %get-tuple-element.29.a_ref), custom_call_target="tpu_custom_call" | custom-call | tf_op jit(solution)/shard_map/lower_inverse/pallas_call | solution.py:67
  440.5 5.2 fusion.11
  451.5 52.4 %lower_inverse.3 = f32[512,512]{1,0:T(8,128)S(1)} custom-call(f32[512,512]{1,0:T(8,128)S(1)} %get-tuple-element.41.a_ref), custom_call_target="tpu_custom_call" | custom-call | tf_op jit(solution)/shard_map/lower_inverse/pallas_call | solution.py:67
  503.9 3.6 fusion.2
  507.7 7.1 %fusion.4 = f32[2048,512]{0,1:T(8,128)S(1)} fusion(f32[512,512]{1,0:T(8,128)S(1)} %lower_inverse.3, f32[2048,512]{1,0:T(8,128)S(1)} %fusion.2, f32[512,512]{1,0:T(8,128)S(1)} %get-tuple-element.40, f32[512,512]{1,0:T(8,128)S(1)} %broadcast_in_dim.60, f32[1024,512]{1,0:T(8,128)S(1)} %get-tuple-element.35), kind=kOutput, calls=%fused_computation.6 | convolution fusion | flops 6445596672 | bytes 13631488 | tf_op jit(solution)/shard_map/dot_general | solution.py:149
  525.1 3.7 convolution_convert_fusion.5
  528.9 5.4 fusion.56
  555.7 20.8 %final.4 = (f32[16384,512]{1,0:T(8,128)}, bf16[2,16384,512]{2,1,0:T(8,128)(2,1)}) custom-call(s32[2]{0:T(128)S(1)} %pad_add_fusion.info, bf16[4096,1024]{1,0:T(8,128)(2,1)} %all-gather.15.cloned.1.call-done.x_ref, bf16[1024,1536]{1,0:T(8,128)(2,1)S(1)} %pad_maximum_fusion.m_ref, f32[2048,512]{1,0:T(8,128)} %copy-done.5, f32[2048,512]{1,0:T(8,128)} %copy-done.4, ...), custom_call_target="tpu_custom_call" | custom-call | tf_op jit(solution)/shard_map/final/pallas_call | solution.py:125
  576.5 20.6 %final.5 = (f32[16384,512]{1,0:T(8,128)}, bf16[2,16384,512]{2,1,0:T(8,128)(2,1)}) custom-call(s32[2]{0:T(128)S(1)} %pad_add_fusion.info, bf16[4096,1024]{1,0:T(8,128)(2,1)} %all-gather.13.cloned.1.call-done.x_ref, bf16[1024,1536]{1,0:T(8,128)(2,1)S(1)} %pad_maximum_fusion.m_ref, ...), custom_call_target="tpu_custom_call", output_to_operand_aliasing={{0}: (6, {}), {1}: (7, {})} | custom-call | tf_op jit(solution)/shard_map/final/pallas_call | solution.py:125
  597.1 20.3 %final.6 = (f32[16384,512]{1,0:T(8,128)}, bf16[2,16384,512]{2,1,0:T(8,128)(2,1)}) custom-call(s32[2]{0:T(128)S(1)} %pad_add_fusion.info, bf16[4096,1024]{1,0:T(8,128)(2,1)} %all-gather.11.cloned.1.call-done.x_ref, bf16[1024,1536]{1,0:T(8,128)(2,1)S(1)} %pad_maximum_fusion.m_ref, ...), custom_call_target="tpu_custom_call", output_to_operand_aliasing={{0}: (6, {}), {1}: (7, {})} | custom-call | tf_op jit(solution)/shard_map/final/pallas_call | solution.py:125
  619.4 20.5 %final.7 = (f32[16384,512]{1,0:T(8,128)}, bf16[2,16384,512]{2,1,0:T(8,128)(2,1)}) custom-call(s32[2]{0:T(128)S(1)} %pad_add_fusion.info, bf16[4096,1024]{1,0:T(8,128)(2,1)} %all-gather.7.cloned.1.call-done.x_ref, bf16[1024,1536]{1,0:T(8,128)(2,1)S(1)} %copy-done.3, f32[2048,512]{1,0:T(8,128)} %copy-done.5, ...), custom_call_target="tpu_custom_call", output_to_operand_aliasing={{0}: (6, {}), {1}: (7, {})} | custom-call | tf_op jit(solution)/shard_map/final/pallas_call | solution.py:125
  (106 shorter events, 55.5 us)
Async XLA Ops:
  7.2 183.2 %copy-start = (bf16[1024,1024]{1,0:T(8,128)(2,1)S(1)}, bf16[1024,1024]{1,0:T(8,128)(2,1)}, u32[]{:S(2)}) copy-start(bf16[1024,1024]{1,0:T(8,128)(2,1)} %param.6) | copy-start | bytes 6291460
  7.2 68.4 %all-reduce.4.cloned.1.call-start = ((), (), s32[]{:S(2)}) async-start(), calls=%async_computation.5 | async-start | bytes 2097152 | tf_op jit(solution)/shard_map/psum | solution.py:177
  16.0 358.5 %all-gather.9.cloned.1.call-start = ((), (), s32[]{:S(2)}) async-start(), calls=%async_computation.6 | async-start | bytes 5242880 | tf_op jit(solution)/shard_map/all_gather | solution.py:178
  75.6 480.1 %all-gather.15.cloned.1.call-start = ((), (), s32[]{:S(2)}) async-start(), calls=%async_computation.9 | async-start | bytes 10485760 | tf_op jit(solution)/shard_map/all_gather | solution.py:190
  194.1 382.4 %all-gather.13.cloned.1.call-start = ((), (), s32[]{:S(2)}) async-start(), calls=%async_computation.8 | async-start | bytes 10485760 | tf_op jit(solution)/shard_map/all_gather | solution.py:190
  251.6 345.5 %all-gather.11.cloned.1.call-start = ((), (), s32[]{:S(2)}) async-start(), calls=%async_computation.7 | async-start | bytes 10485760 | tf_op jit(solution)/shard_map/all_gather | solution.py:190
  308.0 309.5 %all-gather.7.cloned.1.call-start = ((), (), s32[]{:S(2)}) async-start(), calls=%async_computation.4 | async-start | bytes 10485760 | tf_op jit(solution)/shard_map/all_gather | solution.py:190
  360.5 3.7 copy-start.23
  360.5 8.2 %copy-start.22 = (f32[512]{0:T(512)S(1)}, f32[512]{0:T(512)}, u32[]{:S(2)}) copy-start(f32[512]{0:T(512)} %param.7) | copy-start | bytes 6148
  387.3 63.9 %copy-start.13 = (f32[1024,1536]{1,0:T(8,128)}, f32[1024,1536]{1,0:T(8,128)S(1)}, u32[]{:S(2)}) copy-start(f32[1024,1536]{1,0:T(8,128)S(1)} %convolution_multiply_fusion) | copy-start | bytes 18874372
  445.7 58.3 %copy-start.7 = (f32[1536,512]{0,1:T(8,128)}, f32[1536,512]{0,1:T(8,128)S(1)}, u32[]{:S(2)}) copy-start(f32[1536,512]{0,1:T(8,128)S(1)} %fusion.11) | copy-start | bytes 9437188
  451.2 52.7 %copy-start.11 = (f32[512,1024]{1,0:T(8,128)}, f32[512,1024]{1,0:T(8,128)S(1)}, u32[]{:S(2)}) copy-start(f32[512,1024]{1,0:T(8,128)S(1)} %fusion.38) | copy-start | bytes 6291460
  518.6 5.2 slice-start
  528.9 5.5 copy-start.8
  528.9 5.5 copy-start.12
  534.4 6.7 %copy-start.18 = (bf16[1024,512]{0,1:T(8,128)(2,1)S(1)}, bf16[1024,512]{0,1:T(8,128)(2,1)}, u32[]{:S(2)}) copy-start(bf16[1024,512]{0,1:T(8,128)(2,1)} %slice.113) | copy-start | bytes 3145732
  545.9 4.7 copy-start.10
  546.0 5.6 copy-start.4
  546.1 6.7 %copy-start.5 = (f32[2048,512]{1,0:T(8,128)}, f32[2048,512]{1,0:T(8,128)S(1)}, u32[]{:S(2)}) copy-start(f32[2048,512]{1,0:T(8,128)S(1)} %get-tuple-element.44.d0_ref) | copy-start | bytes 12582916
  550.5 4.8 copy-start.19
  550.5 4.8 copy-start.20
  550.5 4.8 copy-start.21
  555.7 41.5 %copy-start.2 = (bf16[1024,1536]{1,0:T(8,128)(2,1)}, bf16[1024,1536]{1,0:T(8,128)(2,1)S(1)}, u32[]{:S(2)}) copy-start(bf16[1024,1536]{1,0:T(8,128)(2,1)S(1)} %pad_maximum_fusion.m_ref) | copy-start | bytes 9437188
  619.4 20.5 %copy-start.1 = (bf16[1024,1024]{1,0:T(8,128)(2,1)S(1)}, bf16[1024,1024]{1,0:T(8,128)(2,1)}, u32[]{:S(2)}) copy-start(bf16[1024,1024]{1,0:T(8,128)(2,1)} %param.6) | copy-start | bytes 6291460
  (7 other events, 13.2 us)
Sparse Core Ops, SparseCore 0:
  16.1 59.4 all-reduce.3
  77.1 124.4 all-gather.8
  203.2 56.4 all-gather.14
  261.1 58.2 all-gather.12
  320.8 58.2 all-gather.10
  380.5 58.2 all-gather.6
